TPU v7x, 32 devices: a whole 2x2x4 slice. The times are simulated.
32 devices in a mesh: seq: 8 (over z, y), chan: 4 (over x, core).
Axes of the slice: x: 2, y: 2, z: 4, core: 2. Of those that a mesh axis runs over, the one named last changes fastest.
Arguments:
- proj_in: bfloat16 [3, 1024, 4096], P(None, 'seq', 'chan'), may hold values from -6 to 6
- taps: float32 [3, 3, 4096], P(None, None, 'chan'), may hold values from -3 to 3
- long_filter: float32 [1024, 256], P('seq'), may hold values from -6 to 6
- out_grad: bfloat16 [1024, 4096], P('seq', 'chan'), may hold values from -0.1875 to 0.1875
Outputs:
- input_grad: bfloat16 [3, 1024, 4096], P(None, 'seq', 'chan')
- long_grad: float32 [1024, 256], P('seq', 'chan')
- tap_grad: float32 [3, 3, 4096], P(None, None, 'chan')
All inputs are finite; a program needn't handle non-finite values.
Results may differ from a plain program's by a relative error of at most 0.001.
Values may be sent and summed in bfloat16 or wider, within the bound.
A program may use at most 64 MiB of HBM per device.

v0:
```python
import math
import jax
import jax.numpy as jnp
from jax import lax
from jax.sharding import PartitionSpec as P


def shifted(x, axis, by):
    devices = lax.axis_size(axis)
    pairs = [(i, i + by) for i in range(devices) if 0 <= i + by < devices]
    return lax.ppermute(x, axis, pairs)


def angle_table(left_index, right_index, period):
    product = left_index[:, None] * right_index[None, :] % period
    phase = product.astype(jnp.float32) * (2.0 * math.pi / period)
    return (jnp.cos(phase), jnp.sin(phase))


def contract(pattern, factor_table, operand):
    return jnp.einsum(pattern, factor_table, operand, precision=lax.Precision.HIGHEST)


def steps_of(count):
    return jnp.arange(count, dtype=jnp.int32)


def whole_forward(signal, seq_width):
    tok_rows, stack_count, channels = signal.shape
    period = 2 * seq_width * tok_rows
    narrow = channels // seq_width
    arrived = lax.all_to_all(signal, "seq", split_axis=2, concat_axis=0, tiled=True)
    laid = arrived.reshape(seq_width, tok_rows, stack_count, narrow).transpose(2, 3, 0, 1)
    cos_step, sin_step = angle_table(steps_of(2 * seq_width), steps_of(seq_width), 2 * seq_width)
    real_part = contract("qm,ncmj->ncqj", cos_step, laid)
    imag_part = -contract("qm,ncmj->ncqj", sin_step, laid)
    cos_turn, sin_turn = angle_table(steps_of(2 * seq_width), steps_of(tok_rows), period)
    turned_re = real_part * cos_turn + imag_part * sin_turn
    turned_im = imag_part * cos_turn - real_part * sin_turn
    cos_row, sin_row = angle_table(steps_of(tok_rows), steps_of(tok_rows), tok_rows)
    spec_re = contract("rj,ncqj->ncqr", cos_row, turned_re) + contract(
        "rj,ncqj->ncqr", sin_row, turned_im
    )
    spec_im = contract("rj,ncqj->ncqr", cos_row, turned_im) - contract(
        "rj,ncqj->ncqr", sin_row, turned_re
    )
    return (spec_re, spec_im)


def whole_inverse(spec_re, spec_im, seq_width):
    stack_count, narrow, freq_count, tok_rows = spec_re.shape
    period = 2 * seq_width * tok_rows
    cos_row, sin_row = angle_table(steps_of(tok_rows), steps_of(tok_rows), tok_rows)
    back_re = contract("rj,ncqr->ncqj", cos_row, spec_re) - contract(
        "rj,ncqr->ncqj", sin_row, spec_im
    )
    back_im = contract("rj,ncqr->ncqj", sin_row, spec_re) + contract(
        "rj,ncqr->ncqj", cos_row, spec_im
    )
    cos_turn, sin_turn = angle_table(steps_of(freq_count), steps_of(tok_rows), period)
    turned_re = back_re * cos_turn - back_im * sin_turn
    turned_im = back_re * sin_turn + back_im * cos_turn
    cos_step, sin_step = angle_table(steps_of(seq_width), steps_of(freq_count), freq_count)
    signal = contract("mq,ncqj->ncmj", cos_step, turned_re) - contract(
        "mq,ncqj->ncmj", sin_step, turned_im
    )
    signal = (
        (signal / period).transpose(2, 3, 0, 1).reshape(seq_width * tok_rows, stack_count, narrow)
    )
    return lax.all_to_all(signal, "seq", split_axis=0, concat_axis=2, tiled=True)


def member(values, index, stack_axis):
    return lax.index_in_dim(values, index, stack_axis, keepdims=False)


def shards(proj_in, taps, long_filter, out_grad):
    stream_count, tok_rows, channels = proj_in.shape
    tap_count = taps.shape[1]
    groups = long_filter.shape[1]
    seq_width = lax.axis_size("seq")
    lower_rim = shifted(proj_in[:, tok_rows - (tap_count - 1) :, :], "seq", 1)
    extended = jnp.concatenate([lower_rim, proj_in], axis=1).astype(jnp.float32)
    lagged = [
        extended[:, tap_count - 1 - lag_step : tap_count - 1 - lag_step + tok_rows, :]
        for lag_step in range(tap_count)
    ]
    featured = taps[:, 0, None, :] * lagged[0]
    for lag_step in range(1, tap_count):
        featured = featured + taps[:, lag_step, None, :] * lagged[lag_step]
    query_rows, key_rows, value_rows = (featured[0], featured[1], featured[2])
    mixed_rows = key_rows * value_rows
    upstream = out_grad.astype(jnp.float32)
    conv_grad = upstream * query_rows
    tiled_filter = jnp.tile(long_filter, (1, channels // groups))
    signals = jnp.stack([mixed_rows, conv_grad, tiled_filter], axis=1)
    data_re, data_im = whole_forward(signals, seq_width)
    stack_axis = 0
    mix_re, mix_im = (member(data_re, 0, stack_axis), member(data_im, 0, stack_axis))
    grad_re, grad_im = (member(data_re, 1, stack_axis), member(data_im, 1, stack_axis))
    filt_re, filt_im = (member(data_re, 2, stack_axis), member(data_im, 2, stack_axis))
    conv_re = filt_re * mix_re - filt_im * mix_im
    conv_im = filt_re * mix_im + filt_im * mix_re
    back_re = filt_re * grad_re + filt_im * grad_im
    back_im = filt_re * grad_im - filt_im * grad_re
    corr_re = grad_re * mix_re + grad_im * mix_im
    corr_im = grad_im * mix_re - grad_re * mix_im
    prod_re = jnp.stack([conv_re, back_re, corr_re], axis=stack_axis)
    prod_im = jnp.stack([conv_im, back_im, corr_im], axis=stack_axis)
    outputs = whole_inverse(prod_re, prod_im, seq_width)
    conv_out, mixed_grad = (outputs[:, 0], outputs[:, 1])
    filt_grad = jnp.sum(outputs[:, 2].reshape(tok_rows, channels // groups, groups), axis=1)
    long_grad = lax.psum_scatter(filt_grad, "chan", scatter_dimension=1, tiled=True)
    feature_grad = jnp.stack(
        [upstream * conv_out, mixed_grad * value_rows, mixed_grad * key_rows], axis=0
    )
    upper_rim = shifted(feature_grad[:, : tap_count - 1, :], "seq", -1)
    trailing = jnp.concatenate([feature_grad, upper_rim], axis=1)
    input_grad = taps[:, 0, None, :] * feature_grad
    for lag_step in range(1, tap_count):
        input_grad = (
            input_grad + taps[:, lag_step, None, :] * trailing[:, lag_step : lag_step + tok_rows]
        )
    partial_taps = jnp.stack(
        [jnp.sum(feature_grad * lagged[lag_step], axis=1) for lag_step in range(tap_count)], axis=1
    )
    tap_grad = lax.psum(partial_taps, "seq") / math.sqrt(seq_width * tok_rows)
    return (input_grad.astype(jnp.bfloat16), long_grad, tap_grad)


def solution(mesh):
    return jax.shard_map(
        shards,
        mesh=mesh,
        in_specs=(P(None, "seq", "chan"), P(None, None, "chan"), P("seq", None), P("seq", "chan")),
        out_specs=(P(None, "seq", "chan"), P("seq", "chan"), P(None, None, "chan")),
        check_vma=False,
    )
```

profile of v0, /device:TPU:0, one launch (start us, length us, event | category | flops | bytes accessed | tf_op | source)
XLA Modules:
  0.0 260.6 jit_solution(12826561988551582519)
XLA Ops:
  8.0 4.9 %collective-permute-start = (bf16[3,2,1024]{2,1,0:T(2,128)(2,1)S(1)}, bf16[3,2,1024]{2,1,0:T(2,128)(2,1)S(1)}, u32[]{:S(2)}, u32[]{:S(2)}) collective-permute-start(bf16[3,2,1024]{2,1,0:T(2,128)(2,1)S(1)} %slice.70), channel_id=1, source_target_pairs={{0,4},{4,8},{8,12},{12,16},{16,20},{20,24},{24,28},{1,5},{5,9},{9,... | collective-permute-start | bytes 36872 | tf_op jit(solution)/shard_map/ppermute | solution.py:11
  14.4 2.3 copy.34
  20.7 2.0 maximum_convert_fusion
  22.7 3.2 %multiply_add_fusion = f32[3,128,1024]{1,2,0:T(8,128)S(1)} fusion(f32[3,130,1024]{1,2,0:T(8,128)S(1)} %maximum_convert_fusion, f32[3,1024]{1,0:T(4,128)S(1)} %get-tuple-element.26, f32[3,1024]{1,0:T(4,128)} %get-tuple-element.27, f32[3,1024]{1,0:T(4,128)S(1)} %bitcast.116), kind=kLoop, calls=%fused_computation.57 | loop fusion | flops 1966080 | bytes 6328320 | tf_op jit(solution)/shard_map/add | solution.py:90
  27.1 2.7 %pad_maximum_fusion.3 = f32[128,3,1024]{0,1,2:T(4,128)} fusion(f32[128,1,1024]{0,1,2:T(1,128)S(1)} %bitcast.113, f32[128,1,1024]{0,1,2:T(1,128)S(1)} %bitcast.114, f32[128,1,1024]{0,1,2:T(1,128)S(1)} %bitcast.112), kind=kLoop, calls=%fused_computation.33 | loop fusion | flops 786432 | bytes 3145728 | tf_op jit(solution)/shard_map/stack | solution.py:96
  29.8 4.9 %all-to-all-start = ((f32[128,3,1024]{0,1,2:T(4,128)}), f32[128,3,1024]{0,1,2:T(4,128)}, u32[]{:S(2)}, u32[]{:S(2)}) async-start(f32[128,3,1024]{0,1,2:T(4,128)} %pad_maximum_fusion.3), calls=%async_computation | async-start | bytes 4194304 | tf_op jit(solution)/shard_map/all_to_all | solution.py:32
  34.9 47.8 %all-to-all-done = f32[128,3,1024]{0,1,2:T(4,128)} async-done(((f32[128,3,1024]{0,1,2:T(4,128)}), f32[128,3,1024]{0,1,2:T(4,128)}, u32[]{:S(2)}, u32[]{:S(2)}) %all-to-all-start) | async-done | bytes 1572896 | tf_op jit(solution)/shard_map/all_to_all | solution.py:32
  82.7 5.1 %fusion.41 = f32[3,128,128,16]{2,3,1,0:T(8,128)S(1)} fusion(f32[128,3,8,128]{0,1,3,2:T(4,128)} %bitcast.5), kind=kOutput, calls=%fused_computation.45 | convolution fusion | flops 75499264 | bytes 4718592 | tf_op jit(solution)/shard_map/qm,ncmj->ncqj/dot_general | solution.py:21
  87.8 5.7 %fusion = (f32[3,128,16,128]{3,2,1,0:T(8,128)S(1)}, f32[3,128,16,128]{3,2,1,0:T(8,128)S(1)}) fusion(f32[3,128,128,16]{2,3,1,0:T(8,128)S(1)} %fusion.41, f32[16,128]{1,0:T(8,128)S(1)} %get-tuple-element.28, f32[16,128]{1,0:T(8,128)S(1)} %get-tuple-element.29, f32[128,3,8,128]{0,1,3,2:T(4,128)} %bitcast.5), kind=kOutput, calls=%fused_computation.5 | convolution fusion | flops 81004288 | bytes 11026432 | tf_op jit(solution)/shard_map/qm,ncmj->ncqj/dot_general | solution.py:21
  93.5 3.6 %fusion.18 = f32[3,128,16,128]{3,1,2,0:T(8,128)S(1)} fusion(f32[3,128,16,128]{3,2,1,0:T(8,128)S(1)} %get-tuple-element.13), kind=kOutput, calls=%fused_computation.25 | convolution fusion | flops 1208188928 | bytes 6291456 | tf_op jit(solution)/shard_map/rj,ncqj->ncqr/dot_general | solution.py:21
  97.2 3.9 %fusion.20 = f32[3,128,16,128]{3,1,2,0:T(8,128)S(1)} fusion(f32[3,128,16,128]{3,2,1,0:T(8,128)S(1)} %get-tuple-element.13), kind=kOutput, calls=%fused_computation.27 | convolution fusion | flops 1208188928 | bytes 6291456 | tf_op jit(solution)/shard_map/rj,ncqj->ncqr/dot_general | solution.py:21
  101.1 3.7 %fusion.29 = f32[3,128,16,128]{3,1,2,0:T(8,128)S(1)} fusion(f32[3,128,16,128]{3,1,2,0:T(8,128)S(1)} %fusion.18, f32[3,128,16,128]{3,2,1,0:T(8,128)S(1)} %get-tuple-element.12), kind=kOutput, calls=%fused_computation.35 | convolution fusion | flops 1208975360 | bytes 9437184 | tf_op jit(solution)/shard_map/rj,ncqj->ncqr/dot_general | solution.py:21
  104.8 3.7 %fusion.26 = f32[3,128,16,128]{3,1,2,0:T(8,128)S(1)} fusion(f32[3,128,16,128]{3,1,2,0:T(8,128)S(1)} %fusion.20, f32[3,128,16,128]{3,2,1,0:T(8,128)S(1)} %get-tuple-element.12), kind=kOutput, calls=%fused_computation.34 | convolution fusion | flops 1208975360 | bytes 9437184 | tf_op jit(solution)/shard_map/rj,ncqj->ncqr/dot_general | solution.py:21
  110.9 4.6 %fusion.10 = f32[3,128,16,128]{3,2,1,0:T(8,128)S(1)} fusion(f32[3,128,16,128]{3,1,2,0:T(8,128)S(1)} %pad_maximum_fusion.1), kind=kOutput, calls=%fused_computation.17 | convolution fusion | flops 1208188928 | bytes 6291456 | tf_op jit(solution)/shard_map/rj,ncqr->ncqj/dot_general | solution.py:21
  115.5 4.7 %fusion.12 = f32[3,128,16,128]{3,2,1,0:T(8,128)S(1)} fusion(f32[3,128,16,128]{3,1,2,0:T(8,128)S(1)} %pad_maximum_fusion.1), kind=kOutput, calls=%fused_computation.19 | convolution fusion | flops 1208188928 | bytes 6291456 | tf_op jit(solution)/shard_map/rj,ncqr->ncqj/dot_general | solution.py:21
  120.4 4.8 %fusion.35 = f32[3,128,16,128]{3,2,1,0:T(8,128)S(1)} fusion(f32[3,128,16,128]{3,2,1,0:T(8,128)S(1)} %fusion.10, f32[3,128,16,128]{3,1,2,0:T(8,128)S(1)} %pad_maximum_fusion), kind=kOutput, calls=%fused_computation.37 | convolution fusion | flops 1208975360 | bytes 9437184 | tf_op jit(solution)/shard_map/rj,ncqr->ncqj/dot_general | solution.py:21
  125.2 4.6 %fusion.32 = f32[3,128,16,128]{3,2,1,0:T(8,128)S(1)} fusion(f32[3,128,16,128]{3,2,1,0:T(8,128)S(1)} %fusion.12, f32[3,128,16,128]{3,1,2,0:T(8,128)S(1)} %pad_maximum_fusion), kind=kOutput, calls=%fused_computation.36 | convolution fusion | flops 1208975360 | bytes 9437184 | tf_op jit(solution)/shard_map/rj,ncqr->ncqj/dot_general | solution.py:21
  129.9 2.1 fusion.2
  132.0 3.4 %multiply_bitcast_fusion = f32[8,128,3,128]{1,0,3,2:T(8,128)} fusion(f32[3,128,128,8]{2,3,1,0:T(8,128)S(1)} %fusion.2, f32[3,128,16,128]{3,2,1,0:T(8,128)S(1)} %fusion.35, f32[3,128,16,128]{3,2,1,0:T(8,128)S(1)} %fusion.32, f32[16,128]{1,0:T(8,128)S(1)} %get-tuple-element.28, f32[16,128]{1,0:T(8,128)S(1)} %get-tuple-element.29), kind=kOutput, calls=%fused_computation.52 | convolution fusion | flops 78644992 | bytes 9453568 | tf_op jit(solution)/shard_map/mq,ncqj->ncmj/dot_general | solution.py:21
  135.4 3.6 %copy.67 = f32[8,128,3,128]{3,2,1,0:T(4,128)} copy(f32[8,128,3,128]{1,0,3,2:T(8,128)} %multiply_bitcast_fusion) | data formatting | bytes 3145728 | tf_op jit(solution)/shard_map/reshape | solution.py:68
  138.9 52.2 %all_to_all.30 = f32[1024,3,128]{2,1,0:T(4,128)} all-to-all(f32[1024,3,128]{2,1,0:T(4,128)} %bitcast.106), channel_id=1, replica_groups=mesh['seq'=8,'chan'=4] {'seq'}, dimensions={0} | all-to-all | bytes 3145728 | tf_op jit(solution)/shard_map/all_to_all | solution.py:70
  191.2 2.7 %copy.48 = f32[8,128,3,128]{1,3,0,2:T(8,128)} copy(f32[8,128,3,128]{3,2,1,0:T(4,128)} %bitcast.107) | data formatting | bytes 3145728 | tf_op jit(solution)/shard_map/all_to_all | solution.py:70
  193.9 1.4 fusion.55
  195.3 1.5 fusion.53
  198.1 1.9 copy.49
  201.3 1.9 slice.108
  203.2 1.7 reduce_sum.36
  205.7 1.7 copy.50
  207.4 2.2 pad_maximum_fusion.2
  209.7 5.2 %multiply_reduce_fusion.2 = (f32[3,1024]{1,0:T(4,128)S(1)}, f32[3,1024]{1,0:T(4,128)S(1)}, f32[3,1024]{1,0:T(4,128)S(1)}, bf16[3,128,1024]{1,2,0:T(8,128)(2,1)}) fusion(f32[3,130,1024]{1,2,0:T(8,128)S(1)} %maximum_convert_fusion, f32[1,128,1024]{1,2,0:T(8,128)S(1)} %copy-done.4, f32[1,128,1024]{1,2,0:T(8,128)S(1)} %copy-done.2, ...), kind=kLoop, calls=%fused_computation.51 | loop fusion | flops 5495808 | bytes 10297344 | tf_op jit(solution)/shard_map/reduce_sum | solution.py:125
  214.9 35.7 %psum.7 = f32[3,3,1024]{2,0,1:T(4,128)S(1)} all-reduce(f32[3,3,1024]{2,0,1:T(4,128)S(1)} %pad_maximum_fusion.5), channel_id=1, replica_groups=mesh['seq'=8,'chan'=4] {'seq'}, use_global_device_ids=true, to_apply=%region_5.6 | all-reduce | flops 9216 | bytes 73728 | tf_op jit(solution)/shard_map/psum | solution.py:127
  251.3 2.3 copy.51
  (45 shorter events, 14.6 us)
Async XLA Ops:
  8.0 11.5 %collective-permute-start = (bf16[3,2,1024]{2,1,0:T(2,128)(2,1)S(1)}, bf16[3,2,1024]{2,1,0:T(2,128)(2,1)S(1)}, u32[]{:S(2)}, u32[]{:S(2)}) collective-permute-start(bf16[3,2,1024]{2,1,0:T(2,128)(2,1)S(1)} %slice.70), channel_id=1, source_target_pairs={{0,4},{4,8},{8,12},{12,16},{16,20},{20,24},{24,28},{1,5},{5,9},{9,... | collective-permute-start | bytes 36872 | tf_op jit(solution)/shard_map/ppermute | solution.py:11
  20.7 2.0 copy-start.8
  25.8 1.2 copy-start
  29.8 52.9 %all-to-all-start = ((f32[128,3,1024]{0,1,2:T(4,128)}), f32[128,3,1024]{0,1,2:T(4,128)}, u32[]{:S(2)}, u32[]{:S(2)}) async-start(f32[128,3,1024]{0,1,2:T(4,128)} %pad_maximum_fusion.3), calls=%async_computation | async-start | bytes 4194304 | tf_op jit(solution)/shard_map/all_to_all | solution.py:32
  34.7 218.9 %reduce-scatter.2.cloned.1.call-start = ((), (), s32[]{:S(2)}) async-start(), calls=%async_computation.3 | async-start | bytes 163840 | tf_op jit(solution)/shard_map/reduce_scatter | solution.py:113
  195.3 1.5 copy-start.1
  195.3 2.8 %copy-start.3 = (f32[1,128,1024]{1,2,0:T(8,128)}, f32[1,128,1024]{1,2,0:T(8,128)S(1)}, u32[]{:S(2)}) copy-start(f32[1,128,1024]{1,2,0:T(8,128)S(1)} %get-tuple-element.21) | copy-start | bytes 1572868
  196.8 1.3 copy-start.5
  200.0 5.7 %collective-permute-start.1 = (f32[3,2,1024]{2,1,0:T(2,128)S(1)}, f32[3,2,1024]{2,1,0:T(2,128)S(1)}, u32[]{:S(2)}, u32[]{:S(2)}) collective-permute-start(f32[3,2,1024]{2,1,0:T(2,128)S(1)} %copy.49), channel_id=1, source_target_pairs={{4,0},{8,4},{12,8},{16,12},{20,16},{24,20},{28,24},{5,1},{9,5},{13... | collective-permute-start | bytes 73736 | tf_op jit(solution)/shard_map/ppermute | solution.py:11
  207.4 2.2 copy-start.2
  207.4 2.2 copy-start.4
  207.4 2.3 copy-start.6
  207.4 2.3 copy-start.7
  207.4 2.3 copy-start.9
Sparse Core Ops, SparseCore 0:
  205.0 19.6 reduce-scatter.1
where the time goes:
time: 265 us; the launch traced here: 261 us
  blocking collectives  87.9 us (33%)
  matrix products  49.9 us (19%)
  waiting for transfers between devices  48.6 us (18%)
  local copies, waits for them, and re-layouts  24.4 us (9%)
  other arithmetic  23.9 us (9%)
  between operations  14.6 us (6%)
  starting transfers between devices  11.3 us (4%)
    all_to_all x1, blocking collectives, whole_inverse(): lax.all_to_all(signal, 'seq', split_axis=0, concat_axis=2, tiled=True)  52.2 us
    dot_general x12, matrix products, contract(): jnp.einsum(pattern, factor_table, operand, precision=lax.Precision.HIGHEST)  49.9 us
    all_to_all x1, waiting for transfers between devices, whole_forward(): lax.all_to_all(signal, 'seq', split_axis=2, concat_axis=0, tiled=True)  47.8 us
    psum x1, blocking collectives, shards(): tap_grad = lax.psum(partial_taps, 'seq') / math.sqrt(seq_width * tok_rows)  35.7 us
    unnamed x27, local copies, waits for them, and re-layouts  9.76 us
    ppermute x2, starting transfers between devices, shifted(): return lax.ppermute(x, axis, pairs)  6.16 us
  transfers between devices with their start and end apart: 4, of which 2 were waited for; matrix products, arithmetic and copies ran while one was open for 9% of the time, Pallas kernels for 0%

commit v1 on v0

--- a/solution.py
+++ b/solution.py
@@ -3,6 +3,15 @@
 import jax.numpy as jnp
 from jax import lax
 from jax.sharding import PartitionSpec as P
+
+
+def _update_levels_all(my_data, group_axis):
+    return jnp.concatenate(
+        lax.all_to_all(
+            jnp.stack(jnp.split(my_data, lax.axis_size(group_axis), 0)), group_axis, 0, 0
+        ),
+        2,
+    )
 
 
 def shifted(x, axis, by):
@@ -67,7 +76,7 @@
     signal = (
         (signal / period).transpose(2, 3, 0, 1).reshape(seq_width * tok_rows, stack_count, narrow)
     )
-    return lax.all_to_all(signal, "seq", split_axis=0, concat_axis=2, tiled=True)
+    return _update_levels_all(signal, "seq")
 
 
 def member(values, index, stack_axis):

time: 265 us -> 244 us (0.921)
  blocking collectives: 87.9 us -> 76.6 us
  other arithmetic: 23.9 us -> 18.5 us
    all_to_all x1, blocking collectives: 52.2 us -> 40.7 us  [_update_levels_all(): lax.all_to_all(jnp.stack(jnp.split(my_data, lax.axis_size(group_axis), 0)...]
    reshape x1 -> x0, local copies, waits for them, and re-layouts: 3.57 us -> none  [whole_inverse(): (signal / period).transpose(2, 3, 0, 1)]
    unnamed x27 -> x31, local copies, waits for them, and re-layouts: 9.76 us -> 10.6 us
where the time goes in v1:
time: 244 us; the launch traced here: 240 us
  blocking collectives  76.6 us (31%)
  matrix products  48.8 us (20%)
  waiting for transfers between devices  48.6 us (20%)
  local copies, waits for them, and re-layouts  21.9 us (9%)
  other arithmetic  18.5 us (8%)
  between operations  14.6 us (6%)
  starting transfers between devices  11.3 us (5%)
    dot_general x12, matrix products, contract(): jnp.einsum(pattern, factor_table, operand, precision=lax.Precision.HIGHEST)  48.8 us
    all_to_all x1, waiting for transfers between devices, whole_forward(): lax.all_to_all(signal, 'seq', split_axis=2, concat_axis=0, tiled=True)  47.8 us
    all_to_all x1, blocking collectives, _update_levels_all(): lax.all_to_all(jnp.stack(jnp.split(my_data, lax.axis_size(group_axis), 0)...  40.7 us
    psum x1, blocking collectives, shards(): tap_grad = lax.psum(partial_taps, 'seq') / math.sqrt(seq_width * tok_rows)  35.9 us
    unnamed x31, local copies, waits for them, and re-layouts  10.6 us
    ppermute x2, starting transfers between devices, shifted(): return lax.ppermute(x, axis, pairs)  6.16 us
    reduce_sum x1, other arithmetic, shards(): jnp.sum(feature_grad * lagged[lag_step], axis=1)  5.17 us
    all_to_all x1, starting transfers between devices, whole_forward(): lax.all_to_all(signal, 'seq', split_axis=2, concat_axis=0, tiled=True)  4.88 us
  transfers between devices with their start and end apart: 4, of which 2 were waited for; matrix products, arithmetic and copies ran while one was open for 9% of the time, Pallas kernels for 0%

profile of v1, /device:TPU:0, one launch (start us, length us, event | category | flops | bytes accessed | tf_op | source)
XLA Modules:
  0.0 240.2 jit_solution(8102812210372542458)
XLA Ops:
  8.0 4.9 %collective-permute-start = (bf16[3,2,1024]{2,1,0:T(2,128)(2,1)S(1)}, bf16[3,2,1024]{2,1,0:T(2,128)(2,1)S(1)}, u32[]{:S(2)}, u32[]{:S(2)}) collective-permute-start(bf16[3,2,1024]{2,1,0:T(2,128)(2,1)S(1)} %slice.79), channel_id=1, source_target_pairs={{0,4},{4,8},{8,12},{12,16},{16,20},{20,24},{24,28},{1,5},{5,9},{9,... | collective-permute-start | bytes 36872 | tf_op jit(solution)/shard_map/ppermute | solution.py:20
  14.4 2.3 copy.33
  18.3 1.1 copy.31
  19.5 1.2 copy.32
  20.7 2.0 maximum_convert_fusion
  22.7 3.2 %multiply_add_fusion = f32[3,128,1024]{1,2,0:T(8,128)S(1)} fusion(f32[3,130,1024]{1,2,0:T(8,128)S(1)} %maximum_convert_fusion, f32[3,1024]{1,0:T(4,128)S(1)} %get-tuple-element.26, f32[3,1024]{1,0:T(4,128)} %get-tuple-element.27, f32[3,1024]{1,0:T(4,128)S(1)} %bitcast.110), kind=kLoop, calls=%fused_computation.57 | loop fusion | flops 1966080 | bytes 6328320 | tf_op jit(solution)/shard_map/add | solution.py:99
  27.2 2.4 copy.35
  29.6 4.9 %all-to-all-start = ((f32[128,3,1024]{0,1,2:T(4,128)}), f32[128,3,1024]{0,1,2:T(4,128)}, u32[]{:S(2)}, u32[]{:S(2)}) async-start(f32[128,3,1024]{0,1,2:T(4,128)} %copy.35), calls=%async_computation | async-start | bytes 4194304 | tf_op jit(solution)/shard_map/all_to_all | solution.py:41
  34.8 47.8 %all-to-all-done = f32[128,3,1024]{0,1,2:T(4,128)} async-done(((f32[128,3,1024]{0,1,2:T(4,128)}), f32[128,3,1024]{0,1,2:T(4,128)}, u32[]{:S(2)}, u32[]{:S(2)}) %all-to-all-start) | async-done | bytes 1572896 | tf_op jit(solution)/shard_map/all_to_all | solution.py:41
  82.6 5.1 %fusion.41 = f32[3,128,128,16]{2,3,1,0:T(8,128)S(1)} fusion(f32[128,3,8,128]{0,1,3,2:T(4,128)} %bitcast.4), kind=kOutput, calls=%fused_computation.45 | convolution fusion | flops 75499264 | bytes 4718592 | tf_op jit(solution)/shard_map/qm,ncmj->ncqj/dot_general | solution.py:30
  87.7 5.7 %fusion = (f32[3,128,16,128]{3,2,1,0:T(8,128)S(1)}, f32[3,128,16,128]{3,2,1,0:T(8,128)S(1)}) fusion(f32[3,128,128,16]{2,3,1,0:T(8,128)S(1)} %fusion.41, f32[16,128]{1,0:T(8,128)S(1)} %get-tuple-element.28, f32[16,128]{1,0:T(8,128)S(1)} %get-tuple-element.29, f32[128,3,8,128]{0,1,3,2:T(4,128)} %bitcast.4), kind=kOutput, calls=%fused_computation.5 | convolution fusion | flops 81004288 | bytes 11026432 | tf_op jit(solution)/shard_map/qm,ncmj->ncqj/dot_general | solution.py:30
  93.4 3.6 %fusion.18 = f32[3,128,16,128]{3,1,2,0:T(8,128)S(1)} fusion(f32[3,128,16,128]{3,2,1,0:T(8,128)S(1)} %get-tuple-element.13), kind=kOutput, calls=%fused_computation.25 | convolution fusion | flops 1208188928 | bytes 6291456 | tf_op jit(solution)/shard_map/rj,ncqj->ncqr/dot_general | solution.py:30
  97.0 3.9 %fusion.20 = f32[3,128,16,128]{3,1,2,0:T(8,128)S(1)} fusion(f32[3,128,16,128]{3,2,1,0:T(8,128)S(1)} %get-tuple-element.13), kind=kOutput, calls=%fused_computation.27 | convolution fusion | flops 1208188928 | bytes 6291456 | tf_op jit(solution)/shard_map/rj,ncqj->ncqr/dot_general | solution.py:30
  101.0 3.7 %fusion.29 = f32[3,128,16,128]{3,1,2,0:T(8,128)S(1)} fusion(f32[3,128,16,128]{3,1,2,0:T(8,128)S(1)} %fusion.18, f32[3,128,16,128]{3,2,1,0:T(8,128)S(1)} %get-tuple-element.12), kind=kOutput, calls=%fused_computation.34 | convolution fusion | flops 1208975360 | bytes 9437184 | tf_op jit(solution)/shard_map/rj,ncqj->ncqr/dot_general | solution.py:30
  104.6 3.7 %fusion.26 = f32[3,128,16,128]{3,1,2,0:T(8,128)S(1)} fusion(f32[3,128,16,128]{3,1,2,0:T(8,128)S(1)} %fusion.20, f32[3,128,16,128]{3,2,1,0:T(8,128)S(1)} %get-tuple-element.12), kind=kOutput, calls=%fused_computation.33 | convolution fusion | flops 1208975360 | bytes 9437184 | tf_op jit(solution)/shard_map/rj,ncqj->ncqr/dot_general | solution.py:30
  110.7 4.6 %fusion.10 = f32[3,128,16,128]{3,2,1,0:T(8,128)S(1)} fusion(f32[3,128,16,128]{3,1,2,0:T(8,128)S(1)} %pad_maximum_fusion.1), kind=kOutput, calls=%fused_computation.17 | convolution fusion | flops 1208188928 | bytes 6291456 | tf_op jit(solution)/shard_map/rj,ncqr->ncqj/dot_general | solution.py:30
  115.4 4.7 %fusion.12 = f32[3,128,16,128]{3,2,1,0:T(8,128)S(1)} fusion(f32[3,128,16,128]{3,1,2,0:T(8,128)S(1)} %pad_maximum_fusion.1), kind=kOutput, calls=%fused_computation.19 | convolution fusion | flops 1208188928 | bytes 6291456 | tf_op jit(solution)/shard_map/rj,ncqr->ncqj/dot_general | solution.py:30
  120.3 4.8 %fusion.35 = f32[3,128,16,128]{3,2,1,0:T(8,128)S(1)} fusion(f32[3,128,16,128]{3,2,1,0:T(8,128)S(1)} %fusion.10, f32[3,128,16,128]{3,1,2,0:T(8,128)S(1)} %pad_maximum_fusion), kind=kOutput, calls=%fused_computation.36 | convolution fusion | flops 1208975360 | bytes 9437184 | tf_op jit(solution)/shard_map/rj,ncqr->ncqj/dot_general | solution.py:30
  125.1 4.6 %fusion.32 = f32[3,128,16,128]{3,2,1,0:T(8,128)S(1)} fusion(f32[3,128,16,128]{3,2,1,0:T(8,128)S(1)} %fusion.12, f32[3,128,16,128]{3,1,2,0:T(8,128)S(1)} %pad_maximum_fusion), kind=kOutput, calls=%fused_computation.35 | convolution fusion | flops 1208975360 | bytes 9437184 | tf_op jit(solution)/shard_map/rj,ncqr->ncqj/dot_general | solution.py:30
  129.7 2.1 fusion.2
  131.8 2.2 multiply_bitcast_fusion
  134.4 40.7 %all_to_all.17 = f32[8,128,3,128]{1,3,2,0:T(8,128)S(1)} all-to-all(f32[8,128,3,128]{1,3,2,0:T(8,128)S(1)} %copy.46), channel_id=1, replica_groups=mesh['seq'=8,'chan'=4] {'seq'}, dimensions={0} | all-to-all | bytes 3145728 | tf_op jit(solution)/shard_map/all_to_all | solution.py:10
  176.3 1.2 pad_maximum_fusion.4
  177.5 1.9 copy.48
  179.4 1.3 collective-permute-start.1
  180.7 1.9 slice.117
  182.6 1.7 reduce_sum.36
  185.1 1.7 copy.49
  186.8 2.2 pad_maximum_fusion.2
  189.1 5.2 %multiply_reduce_fusion.2 = (f32[3,1024]{1,0:T(4,128)S(1)}, f32[3,1024]{1,0:T(4,128)S(1)}, f32[3,1024]{1,0:T(4,128)S(1)}, bf16[3,128,1024]{1,2,0:T(8,128)(2,1)}) fusion(f32[3,130,1024]{1,2,0:T(8,128)S(1)} %maximum_convert_fusion, f32[1,128,1024]{1,2,0:T(8,128)S(1)} %copy-done.5, f32[1,128,1024]{1,2,0:T(8,128)S(1)} %copy-done.3, ...), kind=kLoop, calls=%fused_computation.51 | loop fusion | flops 5495808 | bytes 10297344 | tf_op jit(solution)/shard_map/reduce_sum | solution.py:134
  194.3 35.9 %psum.7 = f32[3,3,1024]{2,0,1:T(4,128)S(1)} all-reduce(f32[3,3,1024]{2,0,1:T(4,128)S(1)} %pad_maximum_fusion.5), channel_id=1, replica_groups=mesh['seq'=8,'chan'=4] {'seq'}, use_global_device_ids=true, to_apply=%region_5.6 | all-reduce | flops 9216 | bytes 73728 | tf_op jit(solution)/shard_map/psum | solution.py:136
  230.9 2.3 copy.50
  (50 shorter events, 11.2 us)
Async XLA Ops:
  8.0 11.5 %collective-permute-start = (bf16[3,2,1024]{2,1,0:T(2,128)(2,1)S(1)}, bf16[3,2,1024]{2,1,0:T(2,128)(2,1)S(1)}, u32[]{:S(2)}, u32[]{:S(2)}) collective-permute-start(bf16[3,2,1024]{2,1,0:T(2,128)(2,1)S(1)} %slice.79), channel_id=1, source_target_pairs={{0,4},{4,8},{8,12},{12,16},{16,20},{20,24},{24,28},{1,5},{5,9},{9,... | collective-permute-start | bytes 36872 | tf_op jit(solution)/shard_map/ppermute | solution.py:20
  20.7 2.0 copy-start.10
  25.8 1.2 copy-start
  29.6 52.9 %all-to-all-start = ((f32[128,3,1024]{0,1,2:T(4,128)}), f32[128,3,1024]{0,1,2:T(4,128)}, u32[]{:S(2)}, u32[]{:S(2)}) async-start(f32[128,3,1024]{0,1,2:T(4,128)} %copy.35), calls=%async_computation | async-start | bytes 4194304 | tf_op jit(solution)/shard_map/all_to_all | solution.py:41
  34.5 198.6 %reduce-scatter.2.cloned.1.call-start = ((), (), s32[]{:S(2)}) async-start(), calls=%async_computation.3 | async-start | bytes 163840 | tf_op jit(solution)/shard_map/reduce_scatter | solution.py:122
  134.4 40.9 %copy-start.1 = (f32[3,128,1024]{1,2,0:T(8,128)S(1)}, f32[3,128,1024]{1,2,0:T(8,128)}, u32[]{:S(2)}) copy-start(f32[3,128,1024]{1,2,0:T(8,128)} %copy-done) | copy-start | bytes 4718596
  175.3 2.3 copy-start.8
  175.4 0.9 copy-start.2
  175.4 2.1 copy-start.4
  175.4 2.1 copy-start.6
  179.4 5.7 %collective-permute-start.1 = (f32[3,2,1024]{2,1,0:T(2,128)S(1)}, f32[3,2,1024]{2,1,0:T(2,128)S(1)}, u32[]{:S(2)}, u32[]{:S(2)}) collective-permute-start(f32[3,2,1024]{2,1,0:T(2,128)S(1)} %copy.48), channel_id=1, source_target_pairs={{4,0},{8,4},{12,8},{16,12},{20,16},{24,20},{28,24},{5,1},{9,5},{13... | collective-permute-start | bytes 73736 | tf_op jit(solution)/shard_map/ppermute | solution.py:20
  186.8 2.2 copy-start.3
  186.8 2.2 copy-start.5
  186.8 2.3 copy-start.7
  186.8 2.3 copy-start.9
  186.8 2.3 copy-start.11
Sparse Core Ops, SparseCore 0:
  184.4 19.8 reduce-scatter.1
